TPU v7x, 512 devices: a whole 4x8x8 slice. The times are simulated.
512 devices in a mesh: cls: 64 (over x, z, y_hi), dp: 8 (over y_lo, core).
Axes of the slice: x: 4, y: 8 (y_hi: 2, y_lo: 4; y = y_hi * 4 + y_lo), z: 8, core: 2. Of those that a mesh axis runs over, the one named last changes fastest.
Arguments:
- features: bfloat16 [65536, 512], P(('cls', 'dp')), may hold values from -6 to 6
- labels: int32 [65536], P(('cls', 'dp')), may hold values from 0 to 16383, as said below
- weights: float32 [65536, 512], P('cls'), may hold values from -0.25 to 0.25
- sampled: int32 [16384], P('cls'), may hold values from 0 to 1023, as said below
Outputs:
- sample_loss: float32 [65536], P(('cls', 'dp'))
- weight_grad: float32 [16384, 512], P(('cls', 'dp'))
Inputs may be any that keep to these rules, and one draw needn't show every extreme that they name: The owner of a label is label // 256. In the rows of one device (aligned blocks of 128 rows) exactly one owner receives 4 of the labels and every other owner fewer. `sampled`: each aligned block of 256 entries holds distinct rows of the owner's bank.
All inputs are finite; a program needn't handle non-finite values.
Results may differ from a plain program's by a relative error of at most 0.0038.
Values may be sent and summed in bfloat16 or wider, within the bound.
A program may use at most 64 MiB of HBM per device.

v0:
```python
import math
import jax
import jax.numpy as jnp
from jax import lax
from jax.sharding import PartitionSpec as P

logit_scale = 64.0
margin = 0.35
epsilon = 1e-06


def normalize_rows(matrix):
    squares = jnp.sum(matrix * matrix, axis=1, keepdims=True)
    return lax.rsqrt(squares + epsilon)


def logits_of(feat_block, label_block, class_block, class_ids):
    cosine = jnp.dot(feat_block, class_block.T, preferred_element_type=jnp.float32)
    target_hit = label_block[:, None] == class_ids[None, :]
    logits = logit_scale * (cosine - margin * target_hit.astype(jnp.float32))
    return (logits, target_hit)


def per_device(features, labels, weights, sampled):
    groups = lax.axis_size("cls")
    replicas = lax.axis_size("dp")
    position = lax.axis_index("cls")
    local_rows = features.shape[0]
    feature_width = features.shape[1]
    classes = sampled.shape[0]
    capacity = local_rows // groups + 2
    feat_wide = features.astype(jnp.float32)
    unit_feats = (feat_wide * normalize_rows(feat_wide)).astype(jnp.bfloat16)
    chosen = weights[sampled]
    inverse_norm = normalize_rows(chosen)
    unit_f32 = chosen * inverse_norm
    unit_rows = unit_f32.astype(jnp.bfloat16)
    owner_ids = labels // classes
    column = labels % classes
    owner_hits = (owner_ids[:, None] == jnp.arange(groups, dtype=jnp.int32)[None, :]).astype(
        jnp.int32
    )
    earlier = jnp.cumsum(owner_hits, axis=0) - owner_hits
    ranking = jnp.sum(earlier * owner_hits, axis=1)
    buffer_slot = owner_ids * capacity + ranking
    slot_codes = jnp.arange(local_rows, dtype=jnp.int32) * classes + column
    outgoing = jnp.full((groups * capacity,), -1, jnp.int32).at[buffer_slot].set(slot_codes)
    outgoing = outgoing.reshape(groups, capacity)
    gathered = lax.all_gather(unit_feats, "cls", axis=0, tiled=True)
    group_rows = gathered.shape[0]

    def decode(incoming):
        is_valid = incoming >= 0
        safe_code = jnp.maximum(incoming, 0)
        source_row = (
            jnp.arange(incoming.shape[0], dtype=jnp.int32)[:, None] * local_rows
            + safe_code // classes
        )
        return (is_valid, source_row, safe_code % classes)

    incoming = lax.all_to_all(outgoing, "cls", split_axis=0, concat_axis=0, tiled=True)
    is_valid, source_row, class_col = decode(incoming)
    feat_rows = gathered[source_row].astype(jnp.float32)
    class_rows = unit_rows[class_col].astype(jnp.float32)
    cosine = jnp.sum(feat_rows * class_rows, axis=2)
    values = logit_scale * (cosine - margin)
    replies = lax.all_to_all(values, "cls", split_axis=0, concat_axis=0, tiled=True)
    replies, incoming = (replies, incoming)
    is_valid, source_row, class_col = decode(incoming)
    drop_index = jnp.where(is_valid, source_row, group_rows).reshape(-1)
    label_local = (
        jnp.full((group_rows,), -1, jnp.int32)
        .at[drop_index]
        .set(class_col.reshape(-1), mode="drop")
    )
    block_rows = math.gcd(group_rows, 512)
    count_blocks = group_rows // block_rows
    feat_blocks = gathered.reshape(count_blocks, block_rows, feature_width)
    label_blocks = label_local.reshape(count_blocks, block_rows)
    all_ids = jnp.arange(classes, dtype=jnp.int32)

    def first_pass(operands):
        logits, target_hit = logits_of(operands[0], operands[1], unit_rows, all_ids)
        part_sum = jnp.sum(jnp.exp(logits - logit_scale), axis=1)
        part_target = jnp.sum(jnp.where(target_hit, logits, 0.0), axis=1)
        return (part_sum, part_target)

    part_sum, part_target = lax.map(first_pass, (feat_blocks, label_blocks))
    part_sum = part_sum.reshape(group_rows)
    part_target = part_target.reshape(group_rows)
    own_start = position * local_rows
    totals = lax.psum(part_sum, "cls")
    own_target = replies.reshape(-1)[buffer_slot]
    own_total = lax.dynamic_slice_in_dim(totals, own_start, local_rows)
    sample_loss = logit_scale + jnp.log(own_total) - own_target
    total_blocks = totals.reshape(count_blocks, block_rows)
    class_ids = jnp.arange(lax.axis_size("dp") * (classes // replicas), dtype=jnp.int32)

    def accumulate(running, triple):
        logits, target_hit = logits_of(triple[0], triple[1], unit_rows, class_ids)
        softmax = jnp.exp(logits - logit_scale) / triple[2][:, None]
        grads_low = (logit_scale * (softmax - target_hit.astype(jnp.float32)) / replicas).astype(
            jnp.bfloat16
        )
        return (running + jnp.dot(grads_low.T, triple[0], preferred_element_type=jnp.float32), None)

    start_grad = jnp.zeros(
        (lax.axis_size("dp") * (classes // replicas), feature_width), jnp.float32
    )
    unit_grad, _ = lax.scan(accumulate, start_grad, (feat_blocks, label_blocks, total_blocks))
    radial = jnp.sum(unit_f32 * unit_grad, axis=1, keepdims=True)
    weight_grad = lax.psum_scatter(
        inverse_norm * (unit_grad - unit_f32 * radial), "dp", scatter_dimension=0, tiled=True
    )
    return (sample_loss, weight_grad)


def solution(mesh):
    in_specs = (P(("cls", "dp"), None), P(("cls", "dp")), P("cls", None), P("cls"))
    out_specs = (P(("cls", "dp")), P(("cls", "dp"), None))
    return jax.shard_map(
        per_device, mesh=mesh, in_specs=in_specs, out_specs=out_specs, check_vma=False
    )
```

profile of v0, /device:TPU:16, one launch (start us, length us, event | category | flops | bytes accessed | tf_op | source)
XLA Modules:
  0.0 773.6 jit_solution(14654492984104845493)
XLA Ops:
  8.4 1.7 fusion.41
  12.9 17.2 %all-to-all-start = ((s32[64,1,4]{2,1,0:T(1,128)}), s32[64,1,4]{2,1,0:T(1,128)S(1)}, u32[]{:S(2)}, u32[]{:S(2)}) async-start(s32[64,1,4]{2,1,0:T(1,128)} %bitcast.1), calls=%async_computation | async-start | bytes 65536 | tf_op jit(solution)/shard_map/all_to_all | solution.py:61
  32.8 11.6 %all-to-all-done = s32[64,1,4]{2,1,0:T(1,128)S(1)} async-done(((s32[64,1,4]{2,1,0:T(1,128)}), s32[64,1,4]{2,1,0:T(1,128)S(1)}, u32[]{:S(2)}, u32[]{:S(2)}) %all-to-all-start) | async-done | bytes 1056 | tf_op jit(solution)/shard_map/all_to_all | solution.py:61
  45.1 1.4 scatter_custom_fusion.1
  46.6 159.0 %all-gather.2.cloned.1.call-done = bf16[8192,512]{1,0:T(8,128)(2,1)} async-done(((bf16[128,512]{1,0:T(8,128)(2,1)}), bf16[8192,512]{1,0:T(8,128)(2,1)}) %all-gather.2.cloned.1.call-update) | async-done | bytes 8388624 | tf_op jit(solution)/shard_map/all_gather | solution.py:49
  205.6 44.7 %while.26 = (s32[]{:T(128)}, f32[16,512]{1,0:T(8,128)}, bf16[16,512,512]{2,1,0:T(8,128)(2,1)}, bf16[256,512]{1,0:T(8,128)(2,1)S(1)}, s32[16,512]{1,0:T(8,128)S(1)}, /*index=5*/s32[]{:T(128)}, s32[]{:T(128)}) while((s32[]{:T(128)}, f32[16,512]{1,0:T(8,128)}, bf16[16,512,512]{2,1,0:T(8,128)(2,1)}, bf16[256,512]{1,0:T(8,128)(2,1)S(1)}, ...), condition=%wide.region_8.9_spmd.clone, body=%wide.region_6.8_spmd.clone.sunk | while | flops 135003648 | bytes 798817 | solution.py:88
  205.6 1.4 fusion.63
  207.0 1.3 dynamic_update_slice.9
  208.4 1.4 fusion.63
  209.8 1.3 dynamic_update_slice.9
  211.2 1.4 fusion.63
  212.6 1.3 dynamic_update_slice.9
  213.9 1.4 fusion.63
  216.7 1.4 fusion.63
  219.5 1.4 fusion.63
  222.3 1.4 fusion.63
  223.8 1.3 dynamic_update_slice.9
  225.1 1.4 fusion.63
  227.9 1.4 fusion.63
  230.7 1.4 fusion.63
  233.5 1.4 fusion.63
  236.3 1.4 fusion.63
  239.1 1.4 fusion.63
  241.9 1.4 fusion.63
  244.7 1.4 fusion.63
  247.5 1.4 fusion.63
  251.1 435.4 %psum.7 = f32[8192]{0:T(1024)S(1)} all-reduce(f32[8192]{0:T(1024)S(1)} %bitcast.77), channel_id=1, replica_groups=mesh['cls'=64,'dp'=8] {'cls'}, use_global_device_ids=true, to_apply=%region_9.10 | all-reduce | flops 8192 | bytes 65536 | tf_op jit(solution)/shard_map/psum | solution.py:92
  686.5 47.0 %while.27 = (s32[]{:T(128)}, f32[256,512]{1,0:T(8,128)S(1)}, bf16[16,512,512]{2,1,0:T(8,128)(2,1)}, bf16[256,512]{1,0:T(8,128)(2,1)S(1)}, s32[16,512]{1,0:T(8,12...) while((s32[]{:T(128)}, f32[256,512]{1,0:T(8,128)S(1)}, bf16[16,512,512]{2,1,0:T(8,128)(2,1)}, ...), condition=%wide.region_12.13_spmd.clone, body=%wide.region_11.12_spmd.clone.sunk | while | flops 270008320 | bytes 2373230 | solution.py:110
  687.2 2.1 convolution_add_fusion.2
  690.1 2.1 convolution_add_fusion.2
  693.1 2.1 convolution_add_fusion.2
  696.0 2.2 convolution_add_fusion.2
  698.9 2.1 convolution_add_fusion.2
  701.9 2.2 convolution_add_fusion.2
  704.8 2.1 convolution_add_fusion.2
  707.7 2.1 convolution_add_fusion.2
  710.7 2.1 convolution_add_fusion.2
  713.6 2.2 convolution_add_fusion.2
  716.5 2.1 convolution_add_fusion.2
  719.4 2.2 convolution_add_fusion.2
  722.4 2.2 convolution_add_fusion.2
  725.3 2.3 convolution_add_fusion.2
  728.4 2.2 convolution_add_fusion.2
  731.3 2.1 convolution_add_fusion.2
  734.3 1.7 subtract_multiply_fusion
  738.1 5.7 gather_fusion.1
  744.7 4.6 all-to-all-start.1
  749.4 14.2 %all-to-all-done.1 = f32[64,1,4]{2,1,0:T(1,128)S(1)} async-done(((f32[64,1,4]{2,1,0:T(1,128)}), f32[64,1,4]{2,1,0:T(1,128)S(1)}, u32[]{:S(2)}, u32[]{:S(2)}) %all-to-all-start.1) | async-done | bytes 1056 | tf_op jit(solution)/shard_map/all_to_all | solution.py:67
  (128 shorter events, 43.1 us)
Async XLA Ops:
  7.2 23.7 %copy-start = (f32[1024,512]{1,0:T(8,128)S(1)}, f32[1024,512]{1,0:T(8,128)}, u32[]{:S(2)}) copy-start(f32[1024,512]{1,0:T(8,128)} %param.10) | copy-start | bytes 6291460
  7.2 198.4 %all-gather.2.cloned.1.call-start = ((), (), s32[]{:S(2)}) async-start(), calls=%async_computation.3 | async-start | bytes 8519680 | tf_op jit(solution)/shard_map/all_gather | solution.py:49
  11.2 19.0 %copy-start.4 = (s32[128]{0:T(128)}, s32[128]{0:T(128)S(1)}, u32[]{:S(2)}) copy-start(s32[128]{0:T(128)S(1)} %compare_select_fusion.4) | copy-start | bytes 1540
  12.9 31.5 %all-to-all-start = ((s32[64,1,4]{2,1,0:T(1,128)}), s32[64,1,4]{2,1,0:T(1,128)S(1)}, u32[]{:S(2)}, u32[]{:S(2)}) async-start(s32[64,1,4]{2,1,0:T(1,128)} %bitcast.1), calls=%async_computation | async-start | bytes 65536 | tf_op jit(solution)/shard_map/all_to_all | solution.py:61
  30.2 736.6 %reduce-scatter.2.cloned.1.call-start = ((), (), s32[]{:S(2)}) async-start(), calls=%async_computation.4 | async-start | bytes 589824 | tf_op jit(solution)/shard_map/reduce_scatter | solution.py:112
  32.0 0.6 copy-start.2
  32.1 12.4 %copy-start.3 = (s32[64]{0:T(128)}, s32[64]{0:T(128)S(1)}, u32[]{:S(2)}) copy-start(s32[64]{0:T(128)S(1)} %iota_multiply_fusion) | copy-start | bytes 772
  250.3 0.8 copy-start.1
  733.5 15.9 %copy-start.5 = (s32[128]{0:T(128)S(1)}, s32[128]{0:T(128)}, u32[]{:S(2)}) copy-start(s32[128]{0:T(128)} %copy-done.4) | copy-start | bytes 1540
  744.7 18.9 %all-to-all-start.1 = ((f32[64,1,4]{2,1,0:T(1,128)}), f32[64,1,4]{2,1,0:T(1,128)S(1)}, u32[]{:S(2)}, u32[]{:S(2)}) async-start(f32[64,1,4]{2,1,0:T(1,128)} %bitcast.10), calls=%async_computation.1 | async-start | bytes 65536 | tf_op jit(solution)/shard_map/all_to_all | solution.py:67
Sparse Core Ops, SparseCore 0:
  12.5 193.0 all-gather.1
  736.2 23.3 reduce-scatter.1
where the time goes:
time: 777 us; the launch traced here: 774 us
  blocking collectives  435 us (56%)
  waiting for transfers between devices  185 us (24%)
  matrix products  57.7 us (7%)
  local copies, waits for them, and re-layouts  49.1 us (6%)
  starting transfers between devices  21.9 us (3%)
  between operations  14.4 us (2%)
  other arithmetic  9.74 us (1%)
    psum x1, blocking collectives, per_device(): totals = lax.psum(part_sum, 'cls')  435 us
    all_gather x1, waiting for transfers between devices, per_device(): gathered = lax.all_gather(unit_feats, 'cls', axis=0, tiled=True)  159 us
    dot_general x16, matrix products, accumulate(): jnp.dot(grads_low.T, triple[0], preferred_element_type=jnp.float32)  34.6 us
    dot_general x16, matrix products, logits_of(): jnp.dot(feat_block, class_block.T, preferred_element_type=jnp.float32)  23 us
    dynamic_update_slice x16, local copies, waits for them, and re-layouts, per_device(): part_sum, part_target = lax.map(first_pass, (feat_blocks, label_blocks))  21.5 us
    all_to_all x1, starting transfers between devices, per_device(): lax.all_to_all(outgoing, 'cls', split_axis=0, concat_axis=0, tiled=True)  17.2 us
  transfers between devices with their start and end apart: 4, of which 3 were waited for; matrix products, arithmetic and copies ran while one was open for 2% of the time, Pallas kernels for 0%

commit v1 on v0

--- a/solution.py
+++ b/solution.py
@@ -89,7 +89,7 @@
     part_sum = part_sum.reshape(group_rows)
     part_target = part_target.reshape(group_rows)
     own_start = position * local_rows
-    totals = lax.psum(part_sum, "cls")
+    totals = jnp.sum(lax.all_gather(part_sum, "cls"), axis=0)
     own_target = replies.reshape(-1)[buffer_slot]
     own_total = lax.dynamic_slice_in_dim(totals, own_start, local_rows)
     sample_loss = logit_scale + jnp.log(own_total) - own_target

time: 777 us -> 459 us (0.59)
  blocking collectives: 435 us -> 0 us
  waiting for transfers between devices: 185 us -> 315 us
  local copies, waits for them, and re-layouts: 49.1 us -> 29 us
    psum x1 -> x0, blocking collectives: 435 us -> none  [per_device(): totals = lax.psum(part_sum, 'cls')]
    all_gather x0 -> x1, waiting for transfers between devices: none -> 130 us  [per_device(): totals = jnp.sum(lax.all_gather(part_sum, 'cls'), axis=0)]
    dynamic_update_slice x16, local copies, waits for them, and re-layouts: 21.5 us -> 1 us  [per_device(): part_sum, part_target = lax.map(first_pass, (feat_blocks, label_blocks))]
    dynamic_slice x32, local copies, waits for them, and re-layouts: 11.8 us -> 0.26 us  [per_device(): part_sum, part_target = lax.map(first_pass, (feat_blocks, label_blocks))]
    dynamic_slice x16, local copies, waits for them, and re-layouts: 0.16 us -> 11.6 us  [per_device(): lax.scan(accumulate, start_grad, (feat_blocks, label_blocks, total_blocks))]
  transfers between devices with their start and end apart: 4 -> 5, of which waited for: 3 -> 4; matrix products, arithmetic and copies ran while one was open for 2% -> 4% of each run, Pallas kernels for 0% -> 0%
where the time goes in v1:
time: 459 us; the launch traced here: 457 us
  waiting for transfers between devices  315 us (69%)
  matrix products  57.8 us (13%)
  local copies, waits for them, and re-layouts  29 us (6%)
  starting transfers between devices  26.7 us (6%)
  between operations  14.1 us (3%)
  other arithmetic  13.2 us (3%)
    all_gather x1, waiting for transfers between devices, per_device(): gathered = lax.all_gather(unit_feats, 'cls', axis=0, tiled=True)  159 us
    all_gather x1, waiting for transfers between devices, per_device(): totals = jnp.sum(lax.all_gather(part_sum, 'cls'), axis=0)  130 us
    dot_general x16, matrix products, accumulate(): jnp.dot(grads_low.T, triple[0], preferred_element_type=jnp.float32)  34.7 us
    dot_general x16, matrix products, logits_of(): jnp.dot(feat_block, class_block.T, preferred_element_type=jnp.float32)  23.1 us
    all_to_all x1, starting transfers between devices, per_device(): lax.all_to_all(outgoing, 'cls', split_axis=0, concat_axis=0, tiled=True)  17.2 us
    all_to_all x1, waiting for transfers between devices, per_device(): lax.all_to_all(values, 'cls', split_axis=0, concat_axis=0, tiled=True)  14.2 us
    dynamic_slice x16, local copies, waits for them, and re-layouts, per_device(): lax.scan(accumulate, start_grad, (feat_blocks, label_blocks, total_blocks))  11.6 us
    all_to_all x1, waiting for transfers between devices, per_device(): lax.all_to_all(outgoing, 'cls', split_axis=0, concat_axis=0, tiled=True)  11.6 us
  transfers between devices with their start and end apart: 5, of which 4 were waited for; matrix products, arithmetic and copies ran while one was open for 4% of the time, Pallas kernels for 0%

profile of v1, /device:TPU:16, one launch (start us, length us, event | category | flops | bytes accessed | tf_op | source)
XLA Modules:
  0.0 456.6 jit_solution(17063904155357769199)
XLA Ops:
  7.2 1.2 fusion.40
  8.4 1.7 fusion.41
  12.9 17.2 %all-to-all-start = ((s32[64,1,4]{2,1,0:T(1,128)}), s32[64,1,4]{2,1,0:T(1,128)S(1)}, u32[]{:S(2)}, u32[]{:S(2)}) async-start(s32[64,1,4]{2,1,0:T(1,128)} %bitcast.1), calls=%async_computation | async-start | bytes 65536 | tf_op jit(solution)/shard_map/all_to_all | solution.py:61
  32.8 11.6 %all-to-all-done = s32[64,1,4]{2,1,0:T(1,128)S(1)} async-done(((s32[64,1,4]{2,1,0:T(1,128)}), s32[64,1,4]{2,1,0:T(1,128)S(1)}, u32[]{:S(2)}, u32[]{:S(2)}) %all-to-all-start) | async-done | bytes 1056 | tf_op jit(solution)/shard_map/all_to_all | solution.py:61
  45.0 1.4 scatter_custom_fusion.1
  46.5 159.1 %all-gather.4.cloned.1.call-done = bf16[8192,512]{1,0:T(8,128)(2,1)} async-done(((bf16[128,512]{1,0:T(8,128)(2,1)}), bf16[8192,512]{1,0:T(8,128)(2,1)}) %all-gather.4.cloned.1.call-update) | async-done | bytes 8388624 | tf_op jit(solution)/shard_map/all_gather | solution.py:49
  205.5 24.8 %while.26 = (s32[]{:T(128)}, f32[16,512]{1,0:T(8,128)S(1)}, bf16[16,512,512]{2,1,0:T(8,128)(2,1)}, bf16[256,512]{1,0:T(8,128)(2,1)S(1)}, s32[16,512]{1,0:T(8,128)S(1)}, /*index=5*/s32[]{:T(128)}, s32[]{:T(128)}) while((s32[]{:T(128)}, f32[16,512]{1,0:T(8,128)S(1)}, bf16[16,512,512]{2,1,0:T(8,128)(2,1)}, ...), condition=%wide.region_8.9_spmd.clone, body=%wide.region_6.8_spmd.clone.sunk | while | flops 135003648 | bytes 798817 | solution.py:88
  205.6 1.4 fusion.63
  207.1 1.4 fusion.63
  208.6 1.4 fusion.63
  210.2 1.4 fusion.63
  211.8 1.4 fusion.63
  213.3 1.4 fusion.63
  214.9 1.4 fusion.63
  216.4 1.4 fusion.63
  218.0 1.4 fusion.63
  219.5 1.4 fusion.63
  221.1 1.4 fusion.63
  222.6 1.4 fusion.63
  224.2 1.4 fusion.63
  225.7 1.4 fusion.63
  227.3 1.4 fusion.63
  228.8 1.4 fusion.63
  231.1 130.0 %all-gather.6.cloned.1.call-done = f32[64,1,8192]{2,1,0:T(1,128)} async-done(((f32[1,1,8192]{2,1,0:T(1,128)}), f32[64,1,8192]{2,1,0:T(1,128)}) %all-gather.6.cloned.1.call-update) | async-done | bytes 2097168 | tf_op jit(solution)/shard_map/all_gather | solution.py:92
  361.1 3.4 reduce_sum.69
  365.1 46.9 %while.27 = (s32[]{:T(128)}, f32[256,512]{1,0:T(8,128)S(1)}, bf16[16,512,512]{2,1,0:T(8,128)(2,1)}, bf16[256,512]{1,0:T(8,128)(2,1)S(1)}, s32[16,512]{1,0:T(8,12...) while((s32[]{:T(128)}, f32[256,512]{1,0:T(8,128)S(1)}, bf16[16,512,512]{2,1,0:T(8,128)(2,1)}, ...), condition=%wide.region_12.13_spmd.clone, body=%wide.region_11.12_spmd.clone.sunk | while | flops 270008320 | bytes 2373230 | solution.py:110
  365.8 2.2 convolution_add_fusion.2
  368.7 2.2 convolution_add_fusion.2
  371.7 2.2 convolution_add_fusion.2
  374.6 2.2 convolution_add_fusion.2
  377.5 2.2 convolution_add_fusion.2
  380.4 2.2 convolution_add_fusion.2
  383.4 2.2 convolution_add_fusion.2
  386.3 2.2 convolution_add_fusion.2
  389.2 2.2 convolution_add_fusion.2
  392.1 2.2 convolution_add_fusion.2
  395.0 2.2 convolution_add_fusion.2
  398.0 2.2 convolution_add_fusion.2
  400.9 2.2 convolution_add_fusion.2
  403.8 2.3 convolution_add_fusion.2
  406.9 2.2 convolution_add_fusion.2
  409.8 2.2 convolution_add_fusion.2
  412.9 1.7 subtract_multiply_fusion
  415.4 1.2 gather_fusion.2
  416.7 5.7 %gather_fusion.1 = bf16[256,512]{1,0:T(8,128)(2,1)S(1)} fusion(bf16[8192,512]{1,0:T(8,128)(2,1)} %bitcast.70, s32[1024]{0:T(1024)S(1)} %pad_clamp_fusion.2), kind=kCustom, calls=%fused_computation.1 | custom fusion | bytes 525312 | tf_op jit(solution)/shard_map/gather | solution.py:63
  423.2 9.4 %all-to-all-start.1 = ((f32[64,1,4]{2,1,0:T(1,128)}), f32[64,1,4]{2,1,0:T(1,128)S(1)}, u32[]{:S(2)}, u32[]{:S(2)}) async-start(f32[64,1,4]{2,1,0:T(1,128)} %bitcast.10), calls=%async_computation.1 | async-start | bytes 65536 | tf_op jit(solution)/shard_map/all_to_all | solution.py:67
  432.7 14.2 %all-to-all-done.1 = f32[64,1,4]{2,1,0:T(1,128)S(1)} async-done(((f32[64,1,4]{2,1,0:T(1,128)}), f32[64,1,4]{2,1,0:T(1,128)S(1)}, u32[]{:S(2)}, u32[]{:S(2)}) %all-to-all-start.1) | async-done | bytes 1056 | tf_op jit(solution)/shard_map/all_to_all | solution.py:67
  448.2 1.3 gather_fusion.3
  (129 shorter events, 24.9 us)
Async XLA Ops:
  7.2 23.7 %copy-start = (f32[1024,512]{1,0:T(8,128)S(1)}, f32[1024,512]{1,0:T(8,128)}, u32[]{:S(2)}) copy-start(f32[1024,512]{1,0:T(8,128)} %param.10) | copy-start | bytes 6291460
  7.2 198.4 %all-gather.4.cloned.1.call-start = ((), (), s32[]{:S(2)}) async-start(), calls=%async_computation.3 | async-start | bytes 8519680 | tf_op jit(solution)/shard_map/all_gather | solution.py:49
  11.2 20.8 %copy-start.3 = (s32[128]{0:T(128)}, s32[128]{0:T(128)S(1)}, u32[]{:S(2)}) copy-start(s32[128]{0:T(128)S(1)} %compare_select_fusion.4) | copy-start | bytes 1540
  12.9 31.4 %all-to-all-start = ((s32[64,1,4]{2,1,0:T(1,128)}), s32[64,1,4]{2,1,0:T(1,128)S(1)}, u32[]{:S(2)}, u32[]{:S(2)}) async-start(s32[64,1,4]{2,1,0:T(1,128)} %bitcast.1), calls=%async_computation | async-start | bytes 65536 | tf_op jit(solution)/shard_map/all_to_all | solution.py:61
  30.2 330.9 %all-gather.6.cloned.1.call-start = ((), (), s32[]{:S(2)}) async-start(), calls=%async_computation.5 | async-start | bytes 2129920 | tf_op jit(solution)/shard_map/all_gather | solution.py:92
  32.0 0.6 copy-start.1
  32.1 12.5 %copy-start.2 = (s32[64]{0:T(128)}, s32[64]{0:T(128)S(1)}, u32[]{:S(2)}) copy-start(s32[64]{0:T(128)S(1)} %iota_multiply_fusion) | copy-start | bytes 772
  231.0 219.1 %reduce-scatter.2.cloned.1.call-start = ((), (), s32[]{:S(2)}) async-start(), calls=%async_computation.4 | async-start | bytes 589824 | tf_op jit(solution)/shard_map/reduce_scatter | solution.py:112
  412.0 20.6 %copy-start.4 = (s32[128]{0:T(128)S(1)}, s32[128]{0:T(128)}, u32[]{:S(2)}) copy-start(s32[128]{0:T(128)} %copy-done.3) | copy-start | bytes 1540
  423.2 23.6 %all-to-all-start.1 = ((f32[64,1,4]{2,1,0:T(1,128)}), f32[64,1,4]{2,1,0:T(1,128)S(1)}, u32[]{:S(2)}, u32[]{:S(2)}) async-start(f32[64,1,4]{2,1,0:T(1,128)} %bitcast.10), calls=%async_computation.1 | async-start | bytes 65536 | tf_op jit(solution)/shard_map/all_to_all | solution.py:67
Sparse Core Ops, SparseCore 0:
  12.5 193.0 all-gather.3
  231.2 129.8 all-gather.5
  414.7 27.8 reduce-scatter.1
